TPU v7x, 512 devices: a whole 4x8x8 slice. The times are simulated.
512 devices in a mesh: inp: 128 (over y, z, core), vis: 4 (over x).
Axes of the slice: x: 4, y: 8, z: 8, core: 2. Of those that a mesh axis runs over, the one named last changes fastest.
Arguments:
- samples: bfloat16 [128, 2048, 2048], P('vis', 'inp'), may hold values from -6 to 6
- history: bfloat16 [3, 2048, 2048], P(None, 'inp'), may hold values from -6 to 6
- fir_taps: float32 [4, 2048], replicated, may hold values from -3 to 3
- kept_channels: int32 [128], replicated, may hold values from 0 to 1023, as said below
Outputs:
- visibility: bfloat16 [128, 2048, 2048], P('inp', 'vis')
Inputs may be any that keep to these rules, and one draw needn't show every extreme that they name: `kept_channels`: 128 distinct channel numbers in no particular order; channels 0 and 1023 are always among them.
All inputs are finite; a program needn't handle non-finite values.
Results may differ from a plain program's by a relative error of at most 0.0078.
Values may be sent and summed in bfloat16 or wider, within the bound.
A program may use at most 64 MiB of HBM per device.

v0:
```python
from functools import partial
import math
import jax
import jax.numpy as jnp
from jax import lax
from jax.sharding import PartitionSpec as P

TAPS = 4
CH_DEV = 1


def shifted(value, axis, steps):
    count = lax.axis_size(axis)
    initial, last = (max(0, -steps), min(count, count - steps))
    return lax.ppermute(value, axis, [(source, source + steps) for source in range(initial, last)])


def make_table(kept_channels, sample_count):
    positions = jnp.arange(sample_count, dtype=jnp.int32)
    products = kept_channels[:, None] * positions[None, :] % sample_count
    angles = products.astype(jnp.float32) * (2.0 * math.pi / sample_count)
    norm_scale = 1.0 / math.sqrt(sample_count)
    table = jnp.concatenate([jnp.cos(angles) * norm_scale, -jnp.sin(angles) * norm_scale], axis=0)
    return table.astype(jnp.bfloat16)


def add_frames(running, shard_piece, offset, vis_index, row_count):
    real_part = shard_piece[0]
    imag_part = shard_piece[1]
    stacked = jnp.concatenate([real_part, imag_part], axis=1)
    rotated = jnp.concatenate([-imag_part, real_part], axis=1)
    row_block = lax.dynamic_slice_in_dim(stacked, vis_index * row_count, row_count, 2)
    input_total = stacked.shape[2]
    re_block = jnp.einsum("cfa,cfb->cab", row_block, stacked, preferred_element_type=jnp.float32)
    im_block = jnp.einsum("cfa,cfb->cab", row_block, rotated, preferred_element_type=jnp.float32)
    row_ids = vis_index * row_count + jnp.arange(row_count, dtype=jnp.int32)
    col_ids = jnp.arange(input_total, dtype=jnp.int32)
    contribution = jnp.where(col_ids[None, None, :] >= row_ids[None, :, None], re_block, im_block)
    return contribution


def per_device(samples, history, fir_taps, kept_channels):
    vis_count = lax.axis_size("vis")
    vis_index = lax.axis_index("vis")
    inp_count = lax.axis_size("inp")
    frame_count, input_count, sample_count = samples.shape
    history_len = TAPS - 1
    previous = shifted(samples[frame_count - history_len :], "vis", 1)
    previous = jnp.where(vis_index == 0, history, previous)
    extended = jnp.concatenate([previous, samples], axis=0)
    weighted = fir_taps[0][None, None, :] * extended[0:frame_count].astype(jnp.float32)
    for tap_index in range(1, TAPS):
        weighted = weighted + fir_taps[tap_index][None, None, :] * extended[
            tap_index : tap_index + frame_count
        ].astype(jnp.float32)
    weighted = weighted.astype(jnp.bfloat16)
    dft_table = make_table(kept_channels, sample_count)
    kept_total = kept_channels.shape[0]
    spectra = jnp.einsum(
        "kn,fin->kfi", dft_table, weighted, preferred_element_type=jnp.float32
    ).astype(jnp.bfloat16)
    spectra = spectra.reshape(2, kept_total, frame_count, input_count)
    input_total = input_count * inp_count
    row_count = input_total // vis_count
    frame_total = frame_count * vis_count
    initial = jnp.zeros((CH_DEV, row_count, input_total), jnp.float32)
    correlate = partial(add_frames, vis_index=vis_index, row_count=row_count)
    all_frames = lax.all_gather(spectra, "vis", axis=2, tiled=True)
    channel_data = lax.all_to_all(all_frames, "inp", split_axis=1, concat_axis=3, tiled=True)
    summed = correlate(initial, channel_data, 0)
    return (summed / float(frame_total)).astype(jnp.bfloat16)


def solution(mesh):
    return jax.shard_map(
        per_device,
        mesh=mesh,
        in_specs=(P("vis", "inp", None), P(None, "inp", None), P(), P()),
        out_specs=P("inp", "vis", None),
        check_vma=False,
    )
```

profile of v0, /device:TPU:1, one launch (start us, length us, event | category | flops | bytes accessed | tf_op | source)
XLA Modules:
  0.0 116.5 jit_solution(1827298505399509753)
XLA Ops:
  6.5 0.0 copy-start
  6.5 0.0 all-gather.2.cloned.1.call-start
  6.5 1.1 slice.33
  7.6 4.0 %collective-permute-start = (bf16[3,16,2048]{2,1,0:T(8,128)(2,1)S(1)}, bf16[3,16,2048]{2,1,0:T(8,128)(2,1)S(1)}, u32[]{:S(2)}, u32[]{:S(2)}) collective-permute-start(bf16[3,16,2048]{2,1,0:T(8,128)(2,1)S(1)} %slice.33), channel_id=1, source_target_pairs={{0,1},{1,2},{2,3},{4,5},{5,6},{6,7},{8,9},{9,10},{10,11},{12,13},{... | collective-permute-start | bytes 589832 | tf_op jit(solution)/shard_map/ppermute | solution.py:15
  11.6 5.6 %multiply_convert_fusion.2 = (bf16[128,2048]{1,0:T(8,128)(2,1)S(1)}, bf16[128,2048]{1,0:T(8,128)(2,1)S(1)}) fusion(s32[128]{0:T(128)} %param.7), kind=kLoop, calls=%fused_computation.33 | loop fusion | flops 4980736 | bytes 1049088 | tf_op jit(solution)/shard_map/convert
  17.2 1.5 %fusion.29 = (f32[1,2048]{1,0:T(1,128)S(1)}, f32[1,2048]{1,0:T(1,128)S(1)}, f32[1,2048]{1,0:T(1,128)}, f32[1,2048]{1,0:T(1,128)}) fusion(f32[4,2048]{1,0:T(4,128)} %param.6), kind=kLoop, calls=%fused_computation.46 | loop fusion | bytes 65536 | tf_op jit(solution)/shard_map/slice | solution.py:51
  18.8 0.0 collective-permute-done
  18.8 1.0 broadcast_select_fusion
  19.7 0.0 copy-done
  19.7 2.7 %add_convert_fusion = bf16[32,16,2048]{2,1,0:T(8,128)(2,1)S(1)} fusion(bf16[32,16,2048]{2,1,0:T(8,128)(2,1)S(1)} %copy-done, bf16[3,16,2048]{2,1,0:T(8,128)(2,1)S(1)} %broadcast_select_fusion, f32[2048]{0:T(1024)} %bitcast.36, f32[2048]{0:T(1024)} %bitcast.37, f32[2048]{0:T(1024)S(1)} %bitcast.35, f32[2048]{0:T(1024)S(1)} %bitcast.34), kind=kLoop, calls=%fused_computation.1 | loop fusion | flops 15728640 | bytes 4423680 | tf_op jit(solution)/shard_map/convert_element_type | solution.py:56
  22.5 1.6 %fusion.5 = bf16[256,32,16]{0,1,2:T(8,128)(2,1)S(1)} fusion(bf16[32,16,2048]{2,1,0:T(8,128)(2,1)S(1)} %add_convert_fusion, bf16[128,2048]{1,0:T(8,128)(2,1)S(1)} %get-tuple-element.12, bf16[128,2048]{1,0:T(8,128)(2,1)S(1)} %get-tuple-element.11), kind=kOutput, calls=%fused_computation.16 | convolution fusion | flops 539099136 | bytes 3407872 | tf_op jit(solution)/shard_map/kn,fin->kfi/dot_general | solution.py:59
  24.1 0.1 reshape.47
  24.2 1.0 copy.9
  25.2 0.0 all-gather.2.cloned.1.call-update
  25.2 32.2 %all-gather.2.cloned.1.call-done = bf16[2,128,128,16]{1,3,0,2:T(8,128)(2,1)} async-done(((bf16[2,128,32,16]{1,3,0,2:T(8,128)(2,1)}), bf16[2,128,128,16]{1,3,0,2:T(8,128)(2,1)}) %all-gather.2.cloned.1.call-update) | async-done | bytes 1048592 | tf_op jit(solution)/shard_map/all_gather | solution.py:68
  57.5 3.2 %copy.10 = bf16[2,128,128,16]{2,3,0,1:T(8,128)(2,1)} copy(bf16[2,128,128,16]{1,3,0,2:T(8,128)(2,1)} %all-gather.2.cloned.1.call-done) | data formatting | bytes 2097152 | tf_op jit(solution)/shard_map/all_gather | solution.py:68
  60.7 15.2 %all-to-all-start = ((bf16[2,128,128,16]{2,3,0,1:T(8,128)(2,1)}), bf16[2,128,128,16]{2,3,0,1:T(8,128)(2,1)S(1)}, u32[]{:S(2)}, u32[]{:S(2)}) async-start(bf16[2,128,128,16]{2,3,0,1:T(8,128)(2,1)} %copy.10), calls=%async_computation | async-start | bytes 2097152 | tf_op jit(solution)/shard_map/all_to_all | solution.py:69
  75.9 30.4 %all-to-all-done = bf16[2,128,128,16]{2,3,0,1:T(8,128)(2,1)S(1)} async-done(((bf16[2,128,128,16]{2,3,0,1:T(8,128)(2,1)}), bf16[2,128,128,16]{2,3,0,1:T(8,128)(2,1)S(1)}, u32[]{:S(2)}, u32[]{:S(2)}) %all-to-all-start) | async-done | bytes 1048608 | tf_op jit(solution)/shard_map/all_to_all | solution.py:69
  106.3 0.2 copy.17
  106.5 0.2 fusion.28
  106.7 0.1 bitcast_negate_fusion
  106.8 0.7 fusion.9
  107.5 2.1 %fusion = bf16[1,512,2048]{2,1,0:T(8,128)(2,1)} fusion(f32[512,2048]{1,0:T(8,128)S(1)} %fusion.9, s32[512]{0:T(512)S(1)} %iota_add_fusion, bf16[1,128,2048]{1,2,0:T(8,128)(2,1)S(1)} %bitcast.30, bf16[1,128,2048]{1,2,0:T(8,128)(2,1)S(1)} %bitcast_negate_fusion, s32[]{:T(128)S(6)} %select_n.26, bf16[1,128,2048]{1,2,0:T(8,128)(2,1)S(1)} %bitcast.32), kind=kOutput, calls=%fused_computation.5 | convolution fusion | flops 543686656 | bytes 8390660 | tf_op jit(solution)/shard_map/cfa,cfb->cab/dot_general | solution.py:35
  (1 shorter events, 0.0 us)
Async XLA Ops:
  6.5 13.2 %copy-start = (bf16[32,16,2048]{2,1,0:T(8,128)(2,1)S(1)}, bf16[32,16,2048]{2,1,0:T(8,128)(2,1)}, u32[]{:S(2)}) copy-start(bf16[32,16,2048]{2,1,0:T(8,128)(2,1)} %param.4) | copy-start | bytes 6291460
  6.5 50.9 %all-gather.2.cloned.1.call-start = ((), (), s32[]{:S(2)}) async-start(), calls=%async_computation.1 | async-start | bytes 1310720 | tf_op jit(solution)/shard_map/all_gather | solution.py:68
  7.6 11.1 %collective-permute-start = (bf16[3,16,2048]{2,1,0:T(8,128)(2,1)S(1)}, bf16[3,16,2048]{2,1,0:T(8,128)(2,1)S(1)}, u32[]{:S(2)}, u32[]{:S(2)}) collective-permute-start(bf16[3,16,2048]{2,1,0:T(8,128)(2,1)S(1)} %slice.33), channel_id=1, source_target_pairs={{0,1},{1,2},{2,3},{4,5},{5,6},{6,7},{8,9},{9,10},{10,11},{12,13},{... | collective-permute-start | bytes 589832 | tf_op jit(solution)/shard_map/ppermute | solution.py:15
  60.7 45.6 %all-to-all-start = ((bf16[2,128,128,16]{2,3,0,1:T(8,128)(2,1)}), bf16[2,128,128,16]{2,3,0,1:T(8,128)(2,1)S(1)}, u32[]{:S(2)}, u32[]{:S(2)}) async-start(bf16[2,128,128,16]{2,3,0,1:T(8,128)(2,1)} %copy.10), calls=%async_computation | async-start | bytes 2097152 | tf_op jit(solution)/shard_map/all_to_all | solution.py:69
Sparse Core Ops, SparseCore 0:
  25.4 32.0 all-gather.1
where the time goes:
time: 117 us
  waiting for transfers between devices  62.7 us (54%)
  starting transfers between devices  19.2 us (16%)
  between operations  13.5 us (12%)
  other arithmetic  9.41 us (8%)
  local copies, waits for them, and re-layouts  7.24 us (6%)
  matrix products  4.52 us (4%)
    all_gather x1, waiting for transfers between devices, per_device(): all_frames = lax.all_gather(spectra, 'vis', axis=2, tiled=True)  32.2 us
    all_to_all x1, waiting for transfers between devices, per_device(): lax.all_to_all(all_frames, 'inp', split_axis=1, concat_axis=3, tiled=True)  30.4 us
    all_to_all x1, starting transfers between devices, per_device(): lax.all_to_all(all_frames, 'inp', split_axis=1, concat_axis=3, tiled=True)  15.2 us
    another operation x1, other arithmetic  5.62 us
    ppermute x1, starting transfers between devices, shifted(): lax.ppermute(value, axis, [(source, source + steps) for source in range(i...  3.96 us
    all_gather x1, local copies, waits for them, and re-layouts, per_device(): all_frames = lax.all_gather(spectra, 'vis', axis=2, tiled=True)  3.17 us
    convert_element_type x1, other arithmetic, per_device(): weighted = weighted.astype(jnp.bfloat16)  2.74 us
  transfers between devices with their start and end apart: 3, of which 2 were waited for; matrix products, arithmetic and copies ran while one was open for 6% of the time, Pallas kernels for 0%

commit v1 on v0

--- a/solution.py
+++ b/solution.py
@@ -1,3 +1,4 @@
+import functools
 from functools import partial
 import math
 import jax
@@ -7,6 +8,24 @@
 
 TAPS = 4
 CH_DEV = 1
+
+
+def update_routes_all(work_x, where_dim):
+    k_all = lax.psum(1, axis_name="vis")
+    x_now = map(lambda pp: (pp, (pp + 1) % k_all), range(k_all))
+    u_next = range(k_all)
+    runs = list(x_now)
+    pile = list(map(lambda pp: (pp, (pp - 1) % k_all), u_next))
+    low, z1 = ([work_x], [work_x])
+    for _ in range(k_all // 2):
+        low.append(lax.ppermute(low[-1], axis_name="vis", perm=runs))
+    for _ in range((k_all - 1) // 2):
+        z1.append(lax.ppermute(z1[-1], axis_name="vis", perm=pile))
+    val2 = jnp.concatenate([*low[::-1], *z1[1:]], where_dim)
+    return jnp.roll(val2, (lax.axis_index("vis") - k_all // 2) * work_x.shape[where_dim], where_dim)
+
+
+try_all_core = functools.partial(update_routes_all, where_dim=2)
 
 
 def shifted(value, axis, steps):
@@ -65,7 +84,7 @@
     frame_total = frame_count * vis_count
     initial = jnp.zeros((CH_DEV, row_count, input_total), jnp.float32)
     correlate = partial(add_frames, vis_index=vis_index, row_count=row_count)
-    all_frames = lax.all_gather(spectra, "vis", axis=2, tiled=True)
+    all_frames = try_all_core(spectra)
     channel_data = lax.all_to_all(all_frames, "inp", split_axis=1, concat_axis=3, tiled=True)
     summed = correlate(initial, channel_data, 0)
     return (summed / float(frame_total)).astype(jnp.bfloat16)

time: 117 us -> 95.6 us (0.82)
  waiting for transfers between devices: 62.7 us -> 39.6 us
  starting transfers between devices: 19.2 us -> 34.4 us
  between operations: 13.5 us -> 0.21 us
    all_gather x1 -> x0, waiting for transfers between devices: 32.2 us -> none  [per_device(): all_frames = lax.all_gather(spectra, 'vis', axis=2, tiled=True)]
    ppermute x0 -> x3, waiting for transfers between devices: none -> 9.16 us  [the longest x2 7.92 us: update_routes_all(): low.append(lax.ppermute(low[-1], axis_name='vis', perm=runs))]
    ppermute x0 -> x3, starting transfers between devices: none -> 8.67 us  [the longest x1 4.57 us: update_routes_all(): z1.append(lax.ppermute(z1[-1], axis_name='vis', perm=pile))]
    all_to_all x1, starting transfers between devices: 15.2 us -> 21.8 us  [per_device(): lax.all_to_all(all_frames, 'inp', split_axis=1, concat_axis=3, tiled=True)]
    all_gather x1 -> x0, local copies, waits for them, and re-layouts: 3.17 us -> none  [per_device(): all_frames = lax.all_gather(spectra, 'vis', axis=2, tiled=True)]
    dynamic_slice x0 -> x2, local copies, waits for them, and re-layouts: none -> 2.45 us  [update_routes_all(): jnp.roll(val2, (lax.axis_index('vis') - k_all // 2) * work_x.shape[where_...]
  transfers between devices with their start and end apart: 3 -> 5, of which waited for: 2 -> 4; matrix products, arithmetic and copies ran while one was open for 6% -> 8% of each run, Pallas kernels for 0% -> 0%
where the time goes in v1:
time: 95.6 us; the launch traced here: 94.4 us
  waiting for transfers between devices  39.6 us (41%)
  starting transfers between devices  34.4 us (36%)
  other arithmetic  9.41 us (10%)
  local copies, waits for them, and re-layouts  6.28 us (7%)
  matrix products  4.52 us (5%)
    all_to_all x1, waiting for transfers between devices, per_device(): lax.all_to_all(all_frames, 'inp', split_axis=1, concat_axis=3, tiled=True)  30.4 us
    all_to_all x1, starting transfers between devices, per_device(): lax.all_to_all(all_frames, 'inp', split_axis=1, concat_axis=3, tiled=True)  21.8 us
    ppermute x2, waiting for transfers between devices, update_routes_all(): low.append(lax.ppermute(low[-1], axis_name='vis', perm=runs))  7.92 us
    another operation x1, other arithmetic  5.62 us
    ppermute x1, starting transfers between devices, update_routes_all(): z1.append(lax.ppermute(z1[-1], axis_name='vis', perm=pile))  4.57 us
    ppermute x2, starting transfers between devices, update_routes_all(): low.append(lax.ppermute(low[-1], axis_name='vis', perm=runs))  4.1 us
    ppermute x1, starting transfers between devices, shifted(): lax.ppermute(value, axis, [(source, source + steps) for source in range(i...  3.96 us
    convert_element_type x1, other arithmetic, per_device(): weighted = weighted.astype(jnp.bfloat16)  2.74 us
  transfers between devices with their start and end apart: 5, of which 4 were waited for; matrix products, arithmetic and copies ran while one was open for 8% of the time, Pallas kernels for 0%

profile of v1, /device:TPU:1, one launch (start us, length us, event | category | flops | bytes accessed | tf_op | source)
XLA Modules:
  0.0 94.4 jit_solution(12487439155053262871)
XLA Ops:
  0.0 0.0 copy-start
  0.0 1.1 %slice.33 = bf16[3,16,2048]{2,1,0:T(8,128)(2,1)S(1)} slice(bf16[32,16,2048]{2,1,0:T(8,128)(2,1)} %param.4), slice={[29:32], [0:16], [0:2048]} | slice | bytes 393216 | tf_op jit(solution)/shard_map/slice | solution.py:67
  1.1 4.0 %collective-permute-start = (bf16[3,16,2048]{2,1,0:T(8,128)(2,1)S(1)}, bf16[3,16,2048]{2,1,0:T(8,128)(2,1)S(1)}, u32[]{:S(2)}, u32[]{:S(2)}) collective-permute-start(bf16[3,16,2048]{2,1,0:T(8,128)(2,1)S(1)} %slice.33), channel_id=1, source_target_pairs={{0,1},{1,2},{2,3},{4,5},{5,6},{6,7},{8,9},{9,10},{10,11},{12,13},{... | collective-permute-start | bytes 589832 | tf_op jit(solution)/shard_map/ppermute | solution.py:34
  5.1 5.6 %multiply_convert_fusion.2 = (bf16[128,2048]{1,0:T(8,128)(2,1)S(1)}, bf16[128,2048]{1,0:T(8,128)(2,1)S(1)}) fusion(s32[128]{0:T(128)} %param.7), kind=kLoop, calls=%fused_computation.33 | loop fusion | flops 4980736 | bytes 1049088 | tf_op jit(solution)/shard_map/convert
  10.7 1.6 %fusion.29 = (f32[1,2048]{1,0:T(1,128)S(1)}, f32[1,2048]{1,0:T(1,128)S(1)}, f32[1,2048]{1,0:T(1,128)}, f32[1,2048]{1,0:T(1,128)}) fusion(f32[4,2048]{1,0:T(4,128)} %param.6), kind=kLoop, calls=%fused_computation.55 | loop fusion | bytes 65536 | tf_op jit(solution)/shard_map/slice | solution.py:70
  12.2 0.0 collective-permute-done
  12.3 1.0 %broadcast_select_fusion = bf16[3,16,2048]{2,1,0:T(8,128)(2,1)S(1)} fusion(bf16[3,16,2048]{2,1,0:T(8,128)(2,1)} %param.5, bf16[3,16,2048]{2,1,0:T(8,128)(2,1)S(1)} %collective-permute-done, pred[]{:T(512)S(6)} %eq.8), kind=kLoop, calls=%fused_computation.39 | loop fusion | flops 98304 | bytes 589825 | tf_op jit(solution)/shard_map/jit(_where)/select_n | solution.py:68
  13.2 0.0 copy-done
  13.2 2.7 %add_convert_fusion = bf16[32,16,2048]{2,1,0:T(8,128)(2,1)S(1)} fusion(bf16[32,16,2048]{2,1,0:T(8,128)(2,1)S(1)} %copy-done, bf16[3,16,2048]{2,1,0:T(8,128)(2,1)S(1)} %broadcast_select_fusion, f32[2048]{0:T(1024)} %bitcast.36, f32[2048]{0:T(1024)} %bitcast.37, f32[2048]{0:T(1024)S(1)} %bitcast.35, f32[2048]{0:T(1024)S(1)} %bitcast.34), kind=kLoop, calls=%fused_computation.1 | loop fusion | flops 15728640 | bytes 4423680 | tf_op jit(solution)/shard_map/convert_element_type | solution.py:75
  16.0 1.6 %fusion.5 = bf16[256,32,16]{0,1,2:T(8,128)(2,1)S(1)} fusion(bf16[32,16,2048]{2,1,0:T(8,128)(2,1)S(1)} %add_convert_fusion, bf16[128,2048]{1,0:T(8,128)(2,1)S(1)} %get-tuple-element.12, bf16[128,2048]{1,0:T(8,128)(2,1)S(1)} %get-tuple-element.11), kind=kOutput, calls=%fused_computation.16 | convolution fusion | flops 539099136 | bytes 3407872 | tf_op jit(solution)/shard_map/kn,fin->kfi/dot_general | solution.py:78
  17.6 0.1 reshape.47
  17.7 0.2 copy.12
  17.9 2.2 %collective-permute-start.1 = (bf16[2,128,32,16]{1,3,2,0:T(8,128)(2,1)S(1)}, bf16[2,128,32,16]{1,3,2,0:T(8,128)(2,1)S(1)}, u32[]{:S(2)}, u32[]{:S(2)}) collective-permute-start(bf16[2,128,32,16]{1,3,2,0:T(8,128)(2,1)S(1)} %copy.12), channel_id=1, source_target_pairs={{0,1},{1,2},{2,3},{3,0},{4,5},{5,6},{6,7},{7,4},{8,9},{9,10},{10,1... | collective-permute-start | bytes 786440 | tf_op jit(solution)/shard_map/ppermute | solution.py:21
  20.1 6.1 %collective-permute-done.1 = bf16[2,128,32,16]{1,3,2,0:T(8,128)(2,1)S(1)} collective-permute-done((bf16[2,128,32,16]{1,3,2,0:T(8,128)(2,1)S(1)}, bf16[2,128,32,16]{1,3,2,0:T(8,128)(2,1)S(1)}, u32[]{:S(2)}, u32[]{:S(2)}) %collective-permute-start.1) | collective-permute-done | bytes 262176 | tf_op jit(solution)/shard_map/ppermute | solution.py:21
  26.2 1.9 %collective-permute-start.2 = (bf16[2,128,32,16]{1,3,2,0:T(8,128)(2,1)S(1)}, bf16[2,128,32,16]{1,3,2,0:T(8,128)(2,1)S(1)}, u32[]{:S(2)}, u32[]{:S(2)}) collective-permute-start(bf16[2,128,32,16]{1,3,2,0:T(8,128)(2,1)S(1)} %collective-permute-done.1), channel_id=1, source_target_pairs={{0,1},{1,2},{2,3},{3,0},{4,5},{5,6},{6,7},{7,4},{8,9},{9,10},{10,1... | collective-permute-start | bytes 786440 | tf_op jit(solution)/shard_map/ppermute | solution.py:21
  28.1 4.6 %collective-permute-start.3 = (bf16[2,128,32,16]{1,3,2,0:T(8,128)(2,1)S(1)}, bf16[2,128,32,16]{1,3,2,0:T(8,128)(2,1)S(1)}, u32[]{:S(2)}, u32[]{:S(2)}) collective-permute-start(bf16[2,128,32,16]{1,3,2,0:T(8,128)(2,1)S(1)} %copy.12), channel_id=1, source_target_pairs={{0,3},{1,0},{2,1},{3,2},{4,7},{5,4},{6,5},{7,6},{8,11},{9,8},{10,9... | collective-permute-start | bytes 786440 | tf_op jit(solution)/shard_map/ppermute | solution.py:23
  32.7 1.8 %collective-permute-done.2 = bf16[2,128,32,16]{1,3,2,0:T(8,128)(2,1)S(1)} collective-permute-done((bf16[2,128,32,16]{1,3,2,0:T(8,128)(2,1)S(1)}, bf16[2,128,32,16]{1,3,2,0:T(8,128)(2,1)S(1)}, u32[]{:S(2)}, u32[]{:S(2)}) %collective-permute-start.2) | collective-permute-done | bytes 262176 | tf_op jit(solution)/shard_map/ppermute | solution.py:21
  34.6 0.2 constant_dynamic-update-slice_fusion.5
  34.8 1.2 %collective-permute-done.3 = bf16[2,128,32,16]{1,3,2,0:T(8,128)(2,1)S(1)} collective-permute-done((bf16[2,128,32,16]{1,3,2,0:T(8,128)(2,1)S(1)}, bf16[2,128,32,16]{1,3,2,0:T(8,128)(2,1)S(1)}, u32[]{:S(2)}, u32[]{:S(2)}) %collective-permute-start.3) | collective-permute-done | bytes 262176 | tf_op jit(solution)/shard_map/ppermute | solution.py:23
  36.1 0.2 constant_dynamic-update-slice_fusion.1
  36.4 0.2 constant_dynamic-slice_fusion
  36.6 2.3 %copy.16 = bf16[2,128,128,16]{2,3,0,1:T(8,128)(2,1)} copy(bf16[2,128,128,16]{1,3,2,0:T(8,128)(2,1)S(1)} %constant_dynamic-slice_fusion) | data formatting | bytes 2097152 | tf_op jit(solution)/shard_map/jit(_roll_dynamic)/dynamic_slice | solution.py:25
  38.8 21.8 %all-to-all-start = ((bf16[2,128,128,16]{2,3,0,1:T(8,128)(2,1)}), bf16[2,128,128,16]{2,3,0,1:T(8,128)(2,1)S(1)}, u32[]{:S(2)}, u32[]{:S(2)}) async-start(bf16[2,128,128,16]{2,3,0,1:T(8,128)(2,1)} %copy.16), calls=%async_computation | async-start | bytes 2097152 | tf_op jit(solution)/shard_map/all_to_all | solution.py:88
  60.6 30.4 %all-to-all-done = bf16[2,128,128,16]{2,3,0,1:T(8,128)(2,1)S(1)} async-done(((bf16[2,128,128,16]{2,3,0,1:T(8,128)(2,1)}), bf16[2,128,128,16]{2,3,0,1:T(8,128)(2,1)S(1)}, u32[]{:S(2)}, u32[]{:S(2)}) %all-to-all-start) | async-done | bytes 1048608 | tf_op jit(solution)/shard_map/all_to_all | solution.py:88
  91.0 0.2 copy.25
  91.2 0.2 fusion.28
  91.4 0.1 bitcast_negate_fusion
  91.5 0.7 fusion.9
  92.3 2.1 %fusion = bf16[1,512,2048]{2,1,0:T(8,128)(2,1)} fusion(f32[512,2048]{1,0:T(8,128)S(1)} %fusion.9, s32[512]{0:T(512)S(1)} %iota_add_fusion, bf16[1,128,2048]{1,2,0:T(8,128)(2,1)S(1)} %bitcast.30, bf16[1,128,2048]{1,2,0:T(8,128)(2,1)S(1)} %bitcast_negate_fusion, s32[]{:T(128)S(6)} %select_n.40, bf16[1,128,2048]{1,2,0:T(8,128)(2,1)S(1)} %bitcast.32), kind=kOutput, calls=%fused_computation.5 | convolution fusion | flops 543686656 | bytes 8390660 | tf_op jit(solution)/shard_map/cfa,cfb->cab/dot_general | solution.py:54
  (7 shorter events, 0.2 us)
Async XLA Ops:
  0.0 13.2 %copy-start = (bf16[32,16,2048]{2,1,0:T(8,128)(2,1)S(1)}, bf16[32,16,2048]{2,1,0:T(8,128)(2,1)}, u32[]{:S(2)}) copy-start(bf16[32,16,2048]{2,1,0:T(8,128)(2,1)} %param.4) | copy-start | bytes 6291460
  1.1 11.2 %collective-permute-start = (bf16[3,16,2048]{2,1,0:T(8,128)(2,1)S(1)}, bf16[3,16,2048]{2,1,0:T(8,128)(2,1)S(1)}, u32[]{:S(2)}, u32[]{:S(2)}) collective-permute-start(bf16[3,16,2048]{2,1,0:T(8,128)(2,1)S(1)} %slice.33), channel_id=1, source_target_pairs={{0,1},{1,2},{2,3},{4,5},{5,6},{6,7},{8,9},{9,10},{10,11},{12,13},{... | collective-permute-start | bytes 589832 | tf_op jit(solution)/shard_map/ppermute | solution.py:34
  17.9 8.3 %collective-permute-start.1 = (bf16[2,128,32,16]{1,3,2,0:T(8,128)(2,1)S(1)}, bf16[2,128,32,16]{1,3,2,0:T(8,128)(2,1)S(1)}, u32[]{:S(2)}, u32[]{:S(2)}) collective-permute-start(bf16[2,128,32,16]{1,3,2,0:T(8,128)(2,1)S(1)} %copy.12), channel_id=1, source_target_pairs={{0,1},{1,2},{2,3},{3,0},{4,5},{5,6},{6,7},{7,4},{8,9},{9,10},{10,1... | collective-permute-start | bytes 786440 | tf_op jit(solution)/shard_map/ppermute | solution.py:21
  26.2 8.3 %collective-permute-start.2 = (bf16[2,128,32,16]{1,3,2,0:T(8,128)(2,1)S(1)}, bf16[2,128,32,16]{1,3,2,0:T(8,128)(2,1)S(1)}, u32[]{:S(2)}, u32[]{:S(2)}) collective-permute-start(bf16[2,128,32,16]{1,3,2,0:T(8,128)(2,1)S(1)} %collective-permute-done.1), channel_id=1, source_target_pairs={{0,1},{1,2},{2,3},{3,0},{4,5},{5,6},{6,7},{7,4},{8,9},{9,10},{10,1... | collective-permute-start | bytes 786440 | tf_op jit(solution)/shard_map/ppermute | solution.py:21
  28.1 7.9 %collective-permute-start.3 = (bf16[2,128,32,16]{1,3,2,0:T(8,128)(2,1)S(1)}, bf16[2,128,32,16]{1,3,2,0:T(8,128)(2,1)S(1)}, u32[]{:S(2)}, u32[]{:S(2)}) collective-permute-start(bf16[2,128,32,16]{1,3,2,0:T(8,128)(2,1)S(1)} %copy.12), channel_id=1, source_target_pairs={{0,3},{1,0},{2,1},{3,2},{4,7},{5,4},{6,5},{7,6},{8,11},{9,8},{10,9... | collective-permute-start | bytes 786440 | tf_op jit(solution)/shard_map/ppermute | solution.py:23
  38.8 52.2 %all-to-all-start = ((bf16[2,128,128,16]{2,3,0,1:T(8,128)(2,1)}), bf16[2,128,128,16]{2,3,0,1:T(8,128)(2,1)S(1)}, u32[]{:S(2)}, u32[]{:S(2)}) async-start(bf16[2,128,128,16]{2,3,0,1:T(8,128)(2,1)} %copy.16), calls=%async_computation | async-start | bytes 2097152 | tf_op jit(solution)/shard_map/all_to_all | solution.py:88
